TPU v7x, 512 devices: a whole 4x8x8 slice. The times are simulated.
512 devices in a mesh: req: 32 (over x, z), tp: 16 (over y, core).
Axes of the slice: x: 4, y: 8, z: 8, core: 2. Of those that a mesh axis runs over, the one named last changes fastest.
Arguments:
- hidden: bfloat16 [32768, 2048], P(('req', 'tp')), may hold values from -6 to 6
- ln_gain: float32 [2048], replicated, may hold values from 0.1 to 1.9
- w_qkv: bfloat16 [2048, 3, 2048], P(None, None, 'tp'), may hold values from -0.125 to 0.125
- w_out: bfloat16 [2048, 2048], P('tp'), may hold values from -0.125 to 0.125
- cache_kv: bfloat16 [2, 512, 256, 2048], P(None, 'req', None, 'tp'), may hold values from -6 to 6
- cache_len: int32 [512], P('req'), may hold values from 16 to 256, as said below
- ancestors: int32 [512, 64, 64], P('req'), may hold values from 0 to 1, as said below
- accepted: int32 [512, 8], P('req'), may hold values from 0 to 14, as said below
Outputs:
- attn_proj: bfloat16 [32768, 2048], P(('req', 'tp'))
- kept_kv: bfloat16 [2, 512, 8, 2048], P(None, 'req', None, 'tp')
Inputs may be any that keep to these rules, and one draw needn't show every extreme that they name: `cache_len`: at least one request of the whole batch has exactly 256 cached positions. `ancestors`: entry (r, i, j) is 1 exactly where draft token j is token i or an ancestor of it in request r's tree; a token's parent has a lower index and token 0 is the root. `accepted`: each row holds, in increasing order, the first 8 tokens of a path down from the root of the request's tree, each entry the parent of the next.
All inputs are finite; a program needn't handle non-finite values.
Results may differ from a plain program's by a relative error of at most 0.018.
Values may be sent and summed in bfloat16 or wider, within the bound.
A program may use at most 64 MiB of HBM per device.

v0:
```python
import math
import jax
import jax.numpy as jnp
from jax import lax
from jax.sharding import PartitionSpec as P

HD = 128
KEY_BLOCK = 128


def block_part(queries, keys, values, positions, valid, slopes):
    heads = queries.shape[2]
    keys_four = keys.reshape(keys.shape[0], keys.shape[1], heads, HD)
    values_four = values.reshape(values.shape[0], values.shape[1], heads, HD)
    scores = jnp.einsum(
        "rihd,rjhd->rhij", queries, keys_four, preferred_element_type=jnp.float32
    ) * (1.0 / math.sqrt(HD))
    scores = scores + slopes[None, :, None, None] * positions[:, None, None, :]
    allowed = valid[:, None, :, :]
    scores = jnp.where(allowed, scores, -1e30)
    top = jnp.max(scores, axis=3)
    expo = jnp.where(allowed, jnp.exp(scores - top[..., None]), 0.0)
    total = jnp.sum(expo, axis=3)
    weights = expo.astype(jnp.bfloat16)
    summed = jnp.einsum("rhij,rjhd->rihd", weights, values_four, preferred_element_type=jnp.float32)
    return (top, total, summed)


def combine(first, second):
    top = jnp.maximum(first[0], second[0])
    scale_one = jnp.exp(first[0] - top)
    scale_two = jnp.exp(second[0] - top)
    total = first[1] * scale_one + second[1] * scale_two
    summed = (
        first[2] * jnp.transpose(scale_one, (0, 2, 1))[..., None]
        + second[2] * jnp.transpose(scale_two, (0, 2, 1))[..., None]
    )
    return (top, total, summed)


def cache_sweep(queries, keys, values, lengths, stride, slopes):
    requests, drafts, heads = (queries.shape[0], queries.shape[1], queries.shape[2])
    start_state = (
        jnp.full((requests, heads, drafts), -1e30, jnp.float32),
        jnp.zeros((requests, heads, drafts), jnp.float32),
        jnp.zeros((requests, drafts, heads, HD), jnp.float32),
    )
    count = keys.shape[1] // KEY_BLOCK

    def advance(block_index, state):
        start = block_index * KEY_BLOCK
        key_block = lax.dynamic_slice_in_dim(keys, start, KEY_BLOCK, 1)
        value_block = lax.dynamic_slice_in_dim(values, start, KEY_BLOCK, 1)
        cells = (start + jnp.arange(KEY_BLOCK)) * stride
        valid = (cells[None, :] < lengths[:, None])[:, None, :]
        positions = jnp.broadcast_to(cells.astype(jnp.float32)[None, :], (requests, KEY_BLOCK))
        return combine(state, block_part(queries, key_block, value_block, positions, valid, slopes))

    return lax.fori_loop(0, count, advance, start_state)


def on_device(hidden, ln_gain, w_qkv, w_out, cache_kv, cache_len, ancestors, accepted):
    values_f = hidden.astype(jnp.float32)
    mean = jnp.mean(values_f, axis=1, keepdims=True)
    centered = values_f - mean
    var = jnp.mean(centered * centered, axis=1, keepdims=True)
    normed = (centered * lax.rsqrt(var + 1e-05) * ln_gain[None, :]).astype(jnp.bfloat16)
    width = w_qkv.shape[2]
    heads = width // HD
    flat_weight = w_qkv.reshape(w_qkv.shape[0], 3 * width)
    joined = jnp.dot(
        lax.all_gather(normed, "tp", axis=0, tiled=True),
        flat_weight,
        preferred_element_type=jnp.float32,
    )
    requests = cache_len.shape[0]
    drafts = ancestors.shape[1]
    joined = joined.astype(jnp.bfloat16).reshape(requests, drafts, 3, heads, HD)
    queries = joined[:, :, 0]
    new_keys = joined[:, :, 1].reshape(requests, drafts, width)
    new_values = joined[:, :, 2].reshape(requests, drafts, width)
    head_ids = lax.axis_index("tp") * heads + jnp.arange(heads)
    all_heads = heads * lax.axis_size("tp")
    slopes = jnp.exp2(-8.0 * (head_ids.astype(jnp.float32) + 1.0) / all_heads)
    depth = jnp.sum(ancestors, axis=2) - 1
    draft_pos = (cache_len[:, None] + depth).astype(jnp.float32)
    draft_part = block_part(queries, new_keys, new_values, draft_pos, ancestors == 1, slopes)
    cache_part = cache_sweep(queries, cache_kv[0], cache_kv[1], cache_len, 1, slopes)
    merged = combine(cache_part, draft_part)
    attn = (merged[2] / jnp.transpose(merged[1], (0, 2, 1))[..., None]).astype(jnp.bfloat16)
    attn = attn.reshape(requests * drafts, width)
    attn_proj = lax.psum_scatter(
        jnp.dot(attn, w_out, preferred_element_type=jnp.float32).astype(jnp.bfloat16),
        "tp",
        scatter_dimension=0,
        tiled=True,
    )
    onehot = (accepted[:, :, None] == jnp.arange(drafts)[None, None, :]).astype(jnp.bfloat16)
    kept_keys = jnp.einsum("rad,rdc->rac", onehot, new_keys, preferred_element_type=jnp.float32)
    kept_values = jnp.einsum("rad,rdc->rac", onehot, new_values, preferred_element_type=jnp.float32)
    kept_kv = jnp.stack([kept_keys, kept_values]).astype(jnp.bfloat16)
    return (attn_proj, kept_kv)


def solution(mesh):
    placed = (
        P(("req", "tp"), None),
        P(),
        P(None, None, "tp"),
        P("tp", None),
        P(None, "req", None, "tp"),
        P("req"),
        P("req", None, None),
        P("req", None),
    )
    return jax.shard_map(
        on_device,
        mesh=mesh,
        in_specs=placed,
        out_specs=(P(("req", "tp"), None), P(None, "req", None, "tp")),
        check_vma=False,
    )
```

profile of v0, /device:TPU:2, one launch (start us, length us, event | category | flops | bytes accessed | tf_op | source)
XLA Modules:
  0.0 154.7 jit_solution(12655179019747754380)
XLA Ops:
  7.2 1.2 convert_reduce_fusion
  8.4 1.2 fusion.33
  9.6 1.8 %fusion.35 = bf16[64,2048]{1,0:T(8,128)(2,1)} fusion(bf16[64,2048]{1,0:T(8,128)(2,1)} %param.10, f32[2048]{0:T(1024)} %param.11, f32[64]{0:T(128)S(1)} %add_rsqrt_fusion, f32[64]{0:T(128)S(1)} %broadcast_multiply_fusion), kind=kLoop, calls=%fused_computation.56 | loop fusion | flops 655360 | bytes 532992 | tf_op jit(solution)/shard_map/convert_element_type | solution.py:67
  11.6 1.2 copy.18
  13.2 2.6 %copy.16 = bf16[2048,3,128]{0,2,1:T(8,128)(2,1)} copy(bf16[2048,3,128]{2,0,1:T(8,128)(2,1)} %param.12) | data formatting | bytes 3145728 | tf_op args[2]
  15.9 0.7 broadcast_compare_fusion.1
  16.7 2.7 %slice_bitcast_fusion = (bf16[16,256,128]{2,1,0:T(8,128)(2,1)S(1)}, bf16[16,256,128]{2,1,0:T(8,128)(2,1)}) fusion(bf16[2,16,256,128]{3,2,1,0:T(8,128)(2,1)} %param.14), kind=kLoop, calls=%fused_computation.48 | loop fusion | bytes 4194304 | tf_op jit(solution)/shard_map/squeeze | solution.py:88
  19.4 41.4 %all-gather.2.cloned.1.call-done = bf16[1024,2048]{1,0:T(8,128)(2,1)} async-done(((bf16[64,2048]{1,0:T(8,128)(2,1)}), bf16[1024,2048]{1,0:T(8,128)(2,1)}) %all-gather.2.cloned.1.call-update) | async-done | bytes 4194320 | tf_op jit(solution)/shard_map/all_gather | solution.py:72
  60.8 5.9 %convolution_convert_fusion.1 = bf16[1024,384]{1,0:T(8,128)(2,1)} fusion(bf16[1024,2048]{1,0:T(8,128)(2,1)} %all-gather.2.cloned.1.call-done, bf16[2048,384]{0,1:T(8,128)(2,1)} %bitcast.129), kind=kOutput, calls=%fused_computation.34 | convolution fusion | flops 1611005952 | bytes 6553600 | tf_op jit(solution)/shard_map/dot_general | solution.py:71
  66.7 2.4 %reshape.195 = bf16[16,64,3,1,128]{4,2,1,0,3:T(4,128)(2,1)S(1)} reshape(bf16[1024,384]{1,0:T(8,128)(2,1)} %convolution_convert_fusion.1) | data formatting | bytes 1572864 | tf_op jit(solution)/shard_map/reshape | solution.py:78
  69.2 2.2 %fusion.53 = (bf16[16,64,1,1,128]{4,2,1,0,3:T(2,128)(2,1)}, bf16[16,64,1,1,128]{4,2,1,0,3:T(2,128)(2,1)}, bf16[16,64,1,1,128]{4,2,1,0,3:T(2,128)(2,1)S(1)}) fusion(bf16[16,64,3,1,128]{4,2,1,0,3:T(4,128)(2,1)S(1)} %reshape.195), kind=kLoop, calls=%fused_computation.86 | loop fusion | bytes 1572864 | tf_op jit(solution)/shard_map/slice | solution.py:81
  71.4 0.8 copy-done.4
  72.2 5.6 %while.18 = (s32[]{:T(128)}, f32[16,1,64]{2,0,1:T(8,128)S(1)}, f32[16,1,64]{2,0,1:T(8,128)S(1)}, f32[16,64,1,128]{3,1,0,2:T(8,128)S(1)}, s32[16]{0:T(128)S(1)}, ...) while((s32[]{:T(128)}, f32[16,1,64]{2,0,1:T(8,128)S(1)}, ...), condition=%wide.region_5.6_spmd.clone, body=%wide.region_2.5_spmd.clone.sunk | while | flops 68954632 | bytes 4032779 | solution.py:59
  72.3 1.6 %fusion.68 = (f32[16,64]{1,0:T(8,128)S(1)}, f32[16,64,128]{2,1,0:T(8,128)S(1)}) fusion(f32[128]{0:T(128)S(1)} %convert_multiply_fusion.3, bf16[16,64,1,128]{3,1,0,2:T(8,128)(2,1)S(1)} %get-tuple-element.324, bf16[16,256,128]{2,1,0:T(8,128)(2,1)} %get-tuple-element.323, s32[]{:T(128)S(6)} %select_n.64, pred[16,128]{1,0:T(8,128)(4,1)S(1)} %broadcast_compare_fusion.3), kind=kOutput, calls=%fused_computation.85.clone.1 | convolution fusion | flops 34077696 | bytes 1317380 | tf_op jit(solution)/shard_map/while/body/eval_jaxpr/rihd,rjhd->rhij/dot_general | solution.py:15
  73.9 0.4 fusion.70
  74.4 0.6 fusion.72
  75.1 1.6 %fusion.68 = (f32[16,64]{1,0:T(8,128)S(1)}, f32[16,64,128]{2,1,0:T(8,128)S(1)}) fusion(f32[128]{0:T(128)S(1)} %convert_multiply_fusion.3, bf16[16,64,1,128]{3,1,0,2:T(8,128)(2,1)S(1)} %get-tuple-element.324, bf16[16,256,128]{2,1,0:T(8,128)(2,1)} %get-tuple-element.323, s32[]{:T(128)S(6)} %select_n.64, pred[16,128]{1,0:T(8,128)(4,1)S(1)} %broadcast_compare_fusion.3), kind=kOutput, calls=%fused_computation.85.clone.1 | convolution fusion | flops 34077696 | bytes 1317380 | tf_op jit(solution)/shard_map/while/body/eval_jaxpr/rihd,rjhd->rhij/dot_general | solution.py:15
  77.1 0.6 fusion.72
  77.8 1.6 %fusion.54 = (f32[16,64]{1,0:T(8,128)S(1)}, f32[16,64,64]{1,2,0:T(8,128)S(1)}) fusion(pred[16,64,64]{1,2,0:T(32,128)(4,1)} %broadcast_compare_fusion.1, f32[16,64]{1,0:T(8,128)S(1)} %convert_multiply_fusion.1, bf16[16,64,1,1,128]{4,2,1,0,3:T(2,128)(2,1)} %get-tuple-element.218, bf16[16,64,1,1,128]{4,2,1,0,3:T(2,128)(2,1)} %copy-done.4), kind=kOutput, calls=%fused_computation.87 | convolution fusion | flops 17038336 | bytes 860160 | tf_op jit(solution)/shard_map/rihd,rjhd->rhij/dot_general | solution.py:15
  79.6 0.6 fusion.28
  80.2 3.2 %convolution_convert_fusion = bf16[1024,2048]{1,0:T(8,128)(2,1)} fusion(bf16[1024,128]{1,0:T(8,128)(2,1)S(1)} %bitcast.130, bf16[128,2048]{1,0:T(8,128)(2,1)S(1)} %copy-done), kind=kOutput, calls=%fused_computation.33 | convolution fusion | flops 538968064 | bytes 4980736 | tf_op jit(solution)/shard_map/dot_general | solution.py:93
  83.4 0.7 copy-done.9
  84.9 0.6 pad_maximum_fusion
  85.6 62.3 %reduce-scatter.2.cloned.1.call-done = bf16[64,2048]{1,0:T(8,128)(2,1)} async-done(((bf16[1024,2048]{1,0:T(8,128)(2,1)}), bf16[64,2048]{1,0:T(8,128)(2,1)}) %reduce-scatter.2.cloned.1.call-update) | async-done | bytes 262160 | tf_op jit(solution)/shard_map/reduce_scatter | solution.py:92
  (48 shorter events, 2.3 us)
Async XLA Ops:
  7.2 73.0 %copy-start = (bf16[128,2048]{1,0:T(8,128)(2,1)S(1)}, bf16[128,2048]{1,0:T(8,128)(2,1)}, u32[]{:S(2)}) copy-start(bf16[128,2048]{1,0:T(8,128)(2,1)} %param.13) | copy-start | bytes 1572868
  7.2 5.6 %copy-start.3 = (s32[16,64,64]{2,1,0:T(8,128)S(1)}, s32[16,64,64]{2,1,0:T(8,128)}, u32[]{:S(2)}) copy-start(s32[16,64,64]{2,1,0:T(8,128)} %param.16) | copy-start | bytes 786436
  7.2 53.6 %all-gather.2.cloned.1.call-start = ((), (), s32[]{:S(2)}) async-start(), calls=%async_computation.1 | async-start | bytes 4456448 | tf_op jit(solution)/shard_map/all_gather | solution.py:72
  11.5 136.4 %reduce-scatter.2.cloned.1.call-start = ((), (), s32[]{:S(2)}) async-start(), calls=%async_computation.2 | async-start | bytes 4456448 | tf_op jit(solution)/shard_map/reduce_scatter | solution.py:92
  12.8 3.1 %copy-start.1 = (s32[16,64,64]{1,2,0:T(8,128)}, s32[16,64,64]{1,2,0:T(8,128)S(1)}, u32[]{:S(2)}) copy-start(s32[16,64,64]{1,2,0:T(8,128)S(1)} %copy.18) | copy-start | bytes 786436
  12.8 3.0 %copy-start.8 = (s32[16]{0:T(128)S(1)}, s32[16]{0:T(128)}, u32[]{:S(2)}) copy-start(s32[16]{0:T(128)} %param.15) | copy-start | bytes 196
  71.4 0.8 copy-start.4
  72.2 7.2 %copy-start.2 = (s32[16,64,64]{1,2,0:T(8,128)S(1)}, s32[16,64,64]{1,2,0:T(8,128)}, u32[]{:S(2)}) copy-start(s32[16,64,64]{1,2,0:T(8,128)} %copy-done.1) | copy-start | bytes 786436
  77.8 1.8 %copy-start.5 = (bf16[16,64,1,1,128]{4,2,1,0,3:T(2,128)(2,1)S(1)}, bf16[16,64,1,1,128]{4,2,1,0,3:T(2,128)(2,1)}, u32[]{:S(2)}) copy-start(bf16[16,64,1,1,128]{4,2,1,0,3:T(2,128)(2,1)} %get-tuple-element.217) | copy-start | bytes 786436
  77.8 1.8 %copy-start.7 = (pred[16,64,64]{1,2,0:T(32,128)(4,1)S(1)}, pred[16,64,64]{1,2,0:T(32,128)(4,1)}, u32[]{:S(2)}) copy-start(pred[16,64,64]{1,2,0:T(32,128)(4,1)} %broadcast_compare_fusion.1) | copy-start | bytes 196612
  83.4 0.7 copy-start.9
  83.4 1.1 copy-start.6
Sparse Core Ops, SparseCore 0:
  11.6 49.1 all-gather.1
  83.5 64.3 reduce-scatter.1
where the time goes:
time: 155 us
  waiting for transfers between devices  104 us (67%)
  matrix products  16.2 us (10%)
  between operations  14.3 us (9%)
  local copies, waits for them, and re-layouts  13.1 us (8%)
  other arithmetic  7.15 us (5%)
    reduce_scatter x1, waiting for transfers between devices, on_device(): lax.psum_scatter(jnp.dot(attn, w_out, preferred_element_type=jnp.float32)...  62.3 us
    all_gather x1, waiting for transfers between devices, on_device(): lax.all_gather(normed, 'tp', axis=0, tiled=True)  41.4 us
    dot_general x1, matrix products, on_device(): jnp.dot(lax.all_gather(normed, 'tp', axis=0, tiled=True), flat_weight, pr...  5.92 us
    unnamed x24, local copies, waits for them, and re-layouts  5.73 us
    dot_general x3, matrix products, block_part(): jnp.einsum('rihd,rjhd->rhij', queries, keys_four, preferred_element_type=...  4.81 us
    dot_general x1, matrix products, on_device(): jnp.dot(attn, w_out, preferred_element_type=jnp.float32)  3.18 us
  transfers between devices with their start and end apart: 2, of which 2 were waited for; matrix products, arithmetic and copies ran while one was open for 6% of the time, Pallas kernels for 0%

commit v1 on v0

--- a/solution.py
+++ b/solution.py
@@ -6,6 +6,11 @@
 
 HD = 128
 KEY_BLOCK = 128
+
+
+def gather_by_exchange(x, axis, dim):
+    copies = jnp.concatenate([x] * lax.axis_size(axis), axis=dim)
+    return lax.all_to_all(copies, axis, dim, dim, tiled=True)
 
 
 def block_part(queries, keys, values, positions, valid, slopes):
@@ -69,9 +74,7 @@
     heads = width // HD
     flat_weight = w_qkv.reshape(w_qkv.shape[0], 3 * width)
     joined = jnp.dot(
-        lax.all_gather(normed, "tp", axis=0, tiled=True),
-        flat_weight,
-        preferred_element_type=jnp.float32,
+        gather_by_exchange(normed, "tp", 0), flat_weight, preferred_element_type=jnp.float32
     )
     requests = cache_len.shape[0]
     drafts = ancestors.shape[1]

time: 155 us -> 221 us (1.43)
  the two profiles are of different devices: /device:TPU:2 before, /device:TPU:27 now
where the time goes in v1:
time: 221 us; the launch traced here: 220 us
  waiting for transfers between devices  153 us (69%)
  matrix products  17.2 us (8%)
  other arithmetic  14.5 us (7%)
  between operations  14.4 us (7%)
  local copies, waits for them, and re-layouts  13.7 us (6%)
  starting transfers between devices  7.82 us (4%)
    all_to_all x1, waiting for transfers between devices, gather_by_exchange(): return lax.all_to_all(copies, axis, dim, dim, tiled=True)  86.8 us
    reduce_scatter x1, waiting for transfers between devices, on_device(): lax.psum_scatter(jnp.dot(attn, w_out, preferred_element_type=jnp.float32)...  65.8 us
    unnamed x18, other arithmetic  9.02 us
    all_to_all x1, starting transfers between devices, gather_by_exchange(): return lax.all_to_all(copies, axis, dim, dim, tiled=True)  7.78 us
    unnamed x28, local copies, waits for them, and re-layouts  6.4 us
    dot_general x1, matrix products, on_device(): jnp.dot(gather_by_exchange(normed, 'tp', 0), flat_weight, preferred_eleme...  5.91 us
    dot_general x3, matrix products, block_part(): jnp.einsum('rihd,rjhd->rhij', queries, keys_four, preferred_element_type=...  4.75 us
  transfers between devices with their start and end apart: 2, of which 2 were waited for; matrix products, arithmetic and copies ran while one was open for 4% of the time, Pallas kernels for 0%

profile of v1, /device:TPU:27, one launch (start us, length us, event | category | flops | bytes accessed | tf_op | source)
XLA Modules:
  0.0 220.4 jit_solution(10233503459048538276)
XLA Ops:
  7.2 1.2 convert_reduce_fusion
  8.4 1.2 fusion.33
  9.6 1.1 constant_dynamic-update-slice_fusion.15
  10.7 1.1 constant_dynamic-update-slice_fusion.14
  11.8 1.1 constant_dynamic-update-slice_fusion.13
  13.0 1.1 constant_dynamic-update-slice_fusion.12
  14.1 1.1 constant_dynamic-update-slice_fusion.11
  15.2 1.1 constant_dynamic-update-slice_fusion.10
  16.3 1.1 constant_dynamic-update-slice_fusion.9
  18.9 2.0 copy-done.2
  20.8 7.8 %all-to-all-start = ((bf16[16,64,2048]{2,1,0:T(8,128)(2,1)}), bf16[16,64,2048]{2,1,0:T(8,128)(2,1)}, u32[]{:S(2)}, u32[]{:S(2)}) async-start(bf16[16,64,2048]{2,1,0:T(8,128)(2,1)} %bitcast.131), calls=%async_computation | async-start | bytes 8388608 | tf_op jit(solution)/shard_map/all_to_all | solution.py:13
  29.2 2.7 %copy.16 = bf16[2048,3,128]{0,2,1:T(8,128)(2,1)} copy(bf16[2048,3,128]{2,0,1:T(8,128)(2,1)} %param.12) | data formatting | bytes 3145728 | tf_op args[2]
  32.8 2.7 %slice_bitcast_fusion = (bf16[16,256,128]{2,1,0:T(8,128)(2,1)S(1)}, bf16[16,256,128]{2,1,0:T(8,128)(2,1)}) fusion(bf16[2,16,256,128]{3,2,1,0:T(8,128)(2,1)} %param.14), kind=kLoop, calls=%fused_computation.48 | loop fusion | bytes 4194304 | tf_op jit(solution)/shard_map/squeeze | solution.py:91
  35.5 86.8 %all-to-all-done = bf16[16,64,2048]{2,1,0:T(8,128)(2,1)} async-done(((bf16[16,64,2048]{2,1,0:T(8,128)(2,1)}), bf16[16,64,2048]{2,1,0:T(8,128)(2,1)}, u32[]{:S(2)}, u32[]{:S(2)}) %all-to-all-start) | async-done | bytes 4194336 | tf_op jit(solution)/shard_map/all_to_all | solution.py:13
  122.3 5.9 %convolution_convert_fusion.1 = bf16[1024,384]{1,0:T(8,128)(2,1)} fusion(bf16[1024,2048]{1,0:T(8,128)(2,1)} %bitcast.2, bf16[2048,384]{0,1:T(8,128)(2,1)} %bitcast.132), kind=kOutput, calls=%fused_computation.34 | convolution fusion | flops 1611005952 | bytes 6553600 | tf_op jit(solution)/shard_map/dot_general | solution.py:76
  128.2 2.4 %reshape.197 = bf16[16,64,3,1,128]{4,2,1,0,3:T(4,128)(2,1)S(1)} reshape(bf16[1024,384]{1,0:T(8,128)(2,1)} %convolution_convert_fusion.1) | data formatting | bytes 1572864 | tf_op jit(solution)/shard_map/reshape | solution.py:81
  130.6 2.2 fusion.53
  133.6 5.6 %while.18 = (s32[]{:T(128)}, f32[16,1,64]{2,0,1:T(8,128)S(1)}, f32[16,1,64]{2,0,1:T(8,128)S(1)}, f32[16,64,1,128]{3,1,0,2:T(8,128)S(1)}, s32[16]{0:T(128)S(1)}, ...) while((s32[]{:T(128)}, f32[16,1,64]{2,0,1:T(8,128)S(1)}, ...), condition=%wide.region_5.6_spmd.clone, body=%wide.region_2.5_spmd.clone.sunk | while | flops 68954632 | bytes 4032779 | solution.py:64
  133.7 1.6 fusion.68
  136.5 1.6 fusion.68
  139.2 1.5 fusion.54
  140.9 1.7 fusion.28
  142.6 3.2 %convolution_convert_fusion = bf16[1024,2048]{1,0:T(8,128)(2,1)} fusion(bf16[1024,128]{1,0:T(8,128)(2,1)S(1)} %bitcast.133, bf16[128,2048]{1,0:T(8,128)(2,1)S(1)} %copy-done), kind=kOutput, calls=%fused_computation.33 | convolution fusion | flops 538968064 | bytes 4980736 | tf_op jit(solution)/shard_map/dot_general | solution.py:96
  147.7 65.8 %reduce-scatter.2.cloned.1.call-done = bf16[64,2048]{1,0:T(8,128)(2,1)} async-done(((bf16[1024,2048]{1,0:T(8,128)(2,1)}), bf16[64,2048]{1,0:T(8,128)(2,1)}) %reduce-scatter.2.cloned.1.call-update) | async-done | bytes 262160 | tf_op jit(solution)/shard_map/reduce_scatter | solution.py:95
  (66 shorter events, 7.8 us)
Async XLA Ops:
  7.2 135.4 %copy-start = (bf16[128,2048]{1,0:T(8,128)(2,1)S(1)}, bf16[128,2048]{1,0:T(8,128)(2,1)}, u32[]{:S(2)}) copy-start(bf16[128,2048]{1,0:T(8,128)(2,1)} %param.13) | copy-start | bytes 1572868
  7.2 10.3 %copy-start.1 = (bf16[64,2048]{1,0:T(8,128)(2,1)S(1)}, bf16[64,2048]{1,0:T(8,128)(2,1)}, u32[]{:S(2)}) copy-start(bf16[64,2048]{1,0:T(8,128)(2,1)} %param.10) | copy-start | bytes 786436
  7.2 10.3 %copy-start.5 = (f32[2048]{0:T(1024)S(1)}, f32[2048]{0:T(1024)}, u32[]{:S(2)}) copy-start(f32[2048]{0:T(1024)} %param.11) | copy-start | bytes 24580
  18.8 2.0 copy-start.2
  20.8 7.9 %copy-start.6 = (s32[16,64,64]{2,1,0:T(8,128)S(1)}, s32[16,64,64]{2,1,0:T(8,128)}, u32[]{:S(2)}) copy-start(s32[16,64,64]{2,1,0:T(8,128)} %param.16) | copy-start | bytes 786436
  20.8 101.5 %all-to-all-start = ((bf16[16,64,2048]{2,1,0:T(8,128)(2,1)}), bf16[16,64,2048]{2,1,0:T(8,128)(2,1)}, u32[]{:S(2)}, u32[]{:S(2)}) async-start(bf16[16,64,2048]{2,1,0:T(8,128)(2,1)} %bitcast.131), calls=%async_computation | async-start | bytes 8388608 | tf_op jit(solution)/shard_map/all_to_all | solution.py:13
  28.6 3.4 %copy-start.10 = (s32[16]{0:T(128)S(1)}, s32[16]{0:T(128)}, u32[]{:S(2)}) copy-start(s32[16]{0:T(128)} %param.15) | copy-start | bytes 196
  28.6 184.9 %reduce-scatter.2.cloned.1.call-start = ((), (), s32[]{:S(2)}) async-start(), calls=%async_computation.2 | async-start | bytes 4456448 | tf_op jit(solution)/shard_map/reduce_scatter | solution.py:95
  28.9 3.2 %copy-start.3 = (s32[16,64,64]{1,2,0:T(8,128)}, s32[16,64,64]{1,2,0:T(8,128)S(1)}, u32[]{:S(2)}) copy-start(s32[16,64,64]{1,2,0:T(8,128)S(1)} %copy.18) | copy-start | bytes 786436
  132.8 0.8 copy-start.7
  133.6 7.1 %copy-start.4 = (s32[16,64,64]{1,2,0:T(8,128)S(1)}, s32[16,64,64]{1,2,0:T(8,128)}, u32[]{:S(2)}) copy-start(s32[16,64,64]{1,2,0:T(8,128)} %copy-done.3) | copy-start | bytes 786436
  142.6 3.2 %copy-start.11 = (s32[16,8]{0,1:T(8,128)S(1)}, s32[16,8]{0,1:T(8,128)}, u32[]{:S(2)}) copy-start(s32[16,8]{0,1:T(8,128)} %param.17) | copy-start | bytes 1540
  142.6 3.3 %copy-start.9 = (bf16[16,64,1,1,128]{4,2,1,0,3:T(2,128)(2,1)S(1)}, bf16[16,64,1,1,128]{4,2,1,0,3:T(2,128)(2,1)}, u32[]{:S(2)}) copy-start(bf16[16,64,1,1,128]{4,2,1,0,3:T(2,128)(2,1)} %get-tuple-element.218) | copy-start | bytes 786436
  145.8 1.0 copy-start.8
Sparse Core Ops, SparseCore 0:
  145.9 67.5 reduce-scatter.1
